TPU v7x, 32 devices: a whole 2x2x4 slice. The times are simulated.
32 devices in a mesh: dp: 4 (over y, x), expert: 8 (over z, core).
Axes of the slice: x: 2, y: 2, z: 4, core: 2. Of those that a mesh axis runs over, the one named last changes fastest.
Arguments:
- tokens: bfloat16 [4096, 7168], P(('dp', 'expert')), may hold values from -6 to 6
- route_ids: int32 [4096, 8], P(('dp', 'expert')), may hold values from 0 to 255, as said below
- gate_weights: float32 [4096, 8], P(('dp', 'expert')), may hold values from 0.3 to 1.2
- gate_weight: bfloat16 [8, 7168, 1024], P('expert', 'dp'), may hold values from -0.0625 to 0.0625
- up_weight: bfloat16 [8, 7168, 1024], P('expert', 'dp'), may hold values from -0.0625 to 0.0625
- down_weight: bfloat16 [8, 7168, 1024], P('expert', 'dp'), may hold values from -0.1875 to 0.1875
- cotangent: bfloat16 [4096, 7168], P(('dp', 'expert')), may hold values from -3 to 3
Outputs:
- output: bfloat16 [4096, 7168], P(('dp', 'expert'))
- grad_tokens: bfloat16 [4096, 7168], P(('dp', 'expert'))
- grad_gate: bfloat16 [8, 7168, 1024], P('expert', 'dp')
- grad_up: bfloat16 [8, 7168, 1024], P('expert', 'dp')
- grad_down: bfloat16 [8, 7168, 1024], P('expert', 'dp')
Inputs may be any that keep to these rules, and one draw needn't show every extreme that they name: `route_ids`: each token's 8 numbers are different, and at most one of them is below 8. Among the 128 tokens of one device at most 4 name any one number below 8; for each index of dp, one number below 8 is named by exactly 4 tokens of every device with that index.
All inputs are finite; a program needn't handle non-finite values.
Results may differ from a plain program's by a relative error of at most 0.018.
Values may be sent and summed in bfloat16 or wider, within the bound.
No kernel may reach another device: no remote copies, remote signals or barrier semaphores. Data moves between devices by JAX's collectives and lax.ppermute only.
A program may use at most 128 MiB of HBM per device.

v0:
```python
import jax
import jax.numpy as jnp
from jax import lax
from jax.sharding import PartitionSpec as P

CAP = 4


def contract_last(left, right):
    return lax.dot_general(
        left, right, (((1,), (1,)), ((), ())), preferred_element_type=jnp.float32
    )


def contract_first(left, right):
    return lax.dot_general(
        left, right, (((0,), (0,)), ((), ())), preferred_element_type=jnp.float32
    )


def body(tokens, route_ids, gate_weights, gate_weight, up_weight, down_weight, cotangent):
    experts = lax.axis_size("expert")
    gate_mat = gate_weight[0]
    up_mat = up_weight[0]
    down_mat = down_weight[0]
    slice_width = gate_mat.shape[0]
    hidden_units = gate_mat.shape[1]
    labels = jnp.arange(experts, dtype=jnp.int32)
    matches = route_ids[:, :, None] == labels
    chosen = jnp.any(matches, axis=1).astype(jnp.int32)
    gate_of = jnp.sum(jnp.where(matches, gate_weights[:, :, None], 0.0), axis=1)
    ranks = jnp.cumsum(chosen, axis=0) - chosen
    placed = (chosen[:, :, None] == 1) & (ranks[:, :, None] == jnp.arange(CAP, dtype=jnp.int32))
    placer = placed.astype(jnp.bfloat16)
    slot_gate = jnp.sum(jnp.where(placed, gate_of[:, :, None], 0.0), axis=0)
    send_rows = jnp.einsum(
        "tjc,td->jcd", placer, tokens, preferred_element_type=jnp.float32
    ).astype(jnp.bfloat16)
    picked = jnp.einsum("tjc,td->jcd", placer, cotangent, preferred_element_type=jnp.float32)
    send_grads = (slot_gate[:, :, None] * picked).astype(jnp.bfloat16)
    recv_rows, recv_grads = (
        lax.all_to_all(
            lax.all_to_all(send_rows, "dp", split_axis=2, concat_axis=1, tiled=True),
            "expert",
            split_axis=0,
            concat_axis=0,
            tiled=True,
        ),
        lax.all_to_all(
            lax.all_to_all(send_grads, "dp", split_axis=2, concat_axis=1, tiled=True),
            "expert",
            split_axis=0,
            concat_axis=0,
            tiled=True,
        ),
    )
    layout = recv_rows.shape
    row_count = layout[0] * layout[1]
    flat_rows = recv_rows.reshape(row_count, slice_width)
    flat_grads = recv_grads.reshape(row_count, slice_width)
    row_block = flat_rows
    grad_block = flat_grads
    mine = lax.psum_scatter(
        jnp.concatenate(
            [
                jnp.dot(row_block, gate_mat, preferred_element_type=jnp.float32),
                jnp.dot(row_block, up_mat, preferred_element_type=jnp.float32),
                jnp.dot(grad_block, down_mat, preferred_element_type=jnp.float32),
            ],
            axis=1,
        ).astype(jnp.bfloat16),
        "dp",
        scatter_dimension=0,
        tiled=True,
    ).astype(jnp.float32)
    pre_gate = mine[:, :hidden_units]
    pre_up = mine[:, hidden_units : 2 * hidden_units]
    hidden_grad = mine[:, 2 * hidden_units :]
    squash = jax.nn.sigmoid(pre_gate)
    silu_gate = pre_gate * squash
    hidden = (silu_gate * pre_up).astype(jnp.bfloat16)
    gate_grad = (hidden_grad * pre_up * squash * (1.0 + pre_gate * (1.0 - squash))).astype(
        jnp.bfloat16
    )
    up_grad = (hidden_grad * silu_gate).astype(jnp.bfloat16)
    hidden, gate_grad, up_grad = (hidden, gate_grad, up_grad)
    hidden_part = lax.all_gather(hidden, "dp", axis=0, tiled=True)
    gate_part = lax.all_gather(gate_grad, "dp", axis=0, tiled=True)
    up_part = lax.all_gather(up_grad, "dp", axis=0, tiled=True)
    row_block = flat_rows
    grad_block = flat_grads
    out_part = contract_last(hidden_part, down_mat).astype(jnp.bfloat16)
    input_part = (contract_last(gate_part, gate_mat) + contract_last(up_part, up_mat)).astype(
        jnp.bfloat16
    )
    out_rows = out_part
    input_rows = input_part
    gate_total = contract_first(row_block, gate_part)
    up_total = contract_first(row_block, up_part)
    down_total = contract_first(grad_block, hidden_part)
    carry = (out_rows, input_rows, gate_total, up_total, down_total)
    out_rows, input_rows, gate_total, up_total, down_total = carry
    got_out, got_input = (
        lax.all_to_all(
            lax.all_to_all(out_rows.reshape(layout), "dp", split_axis=1, concat_axis=2, tiled=True),
            "expert",
            split_axis=0,
            concat_axis=0,
            tiled=True,
        ),
        lax.all_to_all(
            lax.all_to_all(
                input_rows.reshape(layout), "dp", split_axis=1, concat_axis=2, tiled=True
            ),
            "expert",
            split_axis=0,
            concat_axis=0,
            tiled=True,
        ),
    )
    weighted = slot_gate[:, :, None] * got_out.astype(jnp.float32)
    output = jnp.einsum(
        "tjc,jcd->td", placed.astype(jnp.float32), weighted, precision=lax.Precision.HIGHEST
    ).astype(jnp.bfloat16)
    grad_tokens = jnp.einsum(
        "tjc,jcd->td", placer, got_input, preferred_element_type=jnp.float32
    ).astype(jnp.bfloat16)
    return (
        output,
        grad_tokens,
        gate_total.astype(jnp.bfloat16)[None],
        up_total.astype(jnp.bfloat16)[None],
        down_total.astype(jnp.bfloat16)[None],
    )


def solution(mesh):
    return jax.shard_map(
        body,
        mesh=mesh,
        in_specs=(
            P(("dp", "expert"), None),
            P(("dp", "expert"), None),
            P(("dp", "expert"), None),
            P("expert", "dp", None),
            P("expert", "dp", None),
            P("expert", "dp", None),
            P(("dp", "expert"), None),
        ),
        out_specs=(
            P(("dp", "expert"), None),
            P(("dp", "expert"), None),
            P("expert", "dp", None),
            P("expert", "dp", None),
            P("expert", "dp", None),
        ),
        check_vma=False,
    )
```

profile of v0, /device:TPU:0, one launch (start us, length us, event | category | flops | bytes accessed | tf_op | source)
XLA Modules:
  0.0 243.5 jit_solution(8787925912496322918)
XLA Ops:
  9.1 7.2 %copy.72 = bf16[8,4,7168]{0,1,2:T(4,128)(2,1)} copy(bf16[8,4,7168]{2,0,1:T(8,128)(2,1)S(1)} %convolution_convert_fusion) | data formatting | bytes 917504 | tf_op jit(solution)/shard_map/convert_element_type | solution.py:38
  16.3 10.2 %reshape.53 = bf16[4,2,28672]{2,1,0:T(2,128)(2,1)} reshape(bf16[7168,4,8]{2,1,0:T(4,128)(2,1)} %bitcast.83) | data formatting | bytes 917504
  26.5 5.2 %all-to-all-start = ((bf16[4,2,28672]{2,1,0:T(2,128)(2,1)}), bf16[4,2,28672]{2,1,0:T(2,128)(2,1)S(1)}, u32[]{:S(2)}, u32[]{:S(2)}) async-start(bf16[4,2,28672]{2,1,0:T(2,128)(2,1)} %reshape.53), calls=%async_computation | async-start | bytes 917504 | tf_op jit(solution)/shard_map/all_to_all | solution.py:43
  32.2 7.2 %copy.76 = bf16[8,4,7168]{0,1,2:T(4,128)(2,1)} copy(bf16[8,4,7168]{2,0,1:T(8,128)(2,1)S(1)} %fusion.2) | data formatting | bytes 917504 | tf_op jit(solution)/shard_map/convert_element_type | solution.py:40
  39.4 10.1 %reshape.51 = bf16[4,2,28672]{2,1,0:T(2,128)(2,1)} reshape(bf16[7168,4,8]{2,1,0:T(4,128)(2,1)} %bitcast.84) | data formatting | bytes 917504
  49.5 4.2 %all-to-all-start.2 = ((bf16[4,2,28672]{2,1,0:T(2,128)(2,1)}), bf16[4,2,28672]{2,1,0:T(2,128)(2,1)S(1)}, u32[]{:S(2)}, u32[]{:S(2)}) async-start(bf16[4,2,28672]{2,1,0:T(2,128)(2,1)} %reshape.51), calls=%async_computation.2 | async-start | bytes 917504 | tf_op jit(solution)/shard_map/all_to_all | solution.py:50
  53.6 9.8 %reshape.54 = bf16[7168,4,8]{2,1,0:T(4,128)(2,1)} reshape(bf16[4,2,28672]{2,1,0:T(2,128)(2,1)S(1)} %all-to-all-done) | data formatting | bytes 917504
  63.4 8.7 %copy.74 = bf16[8,4,4,1792]{3,0,2,1:T(8,128)(2,1)S(1)} copy(bf16[8,4,4,1792]{0,2,3,1:T(4,128)(2,1)} %bitcast.85) | data formatting | bytes 917504 | tf_op jit(solution)/shard_map/all_to_all | solution.py:43
  73.0 4.9 %all-to-all-start.1 = ((bf16[8,16,1792]{2,1,0:T(8,128)(2,1)}), bf16[8,16,1792]{2,1,0:T(8,128)(2,1)S(1)}, u32[]{:S(2)}, u32[]{:S(2)}) async-start(bf16[8,16,1792]{2,1,0:T(8,128)(2,1)} %copy.75), calls=%async_computation.1 | async-start | bytes 917504 | tf_op jit(solution)/shard_map/all_to_all | solution.py:42
  77.9 9.8 %reshape.52 = bf16[7168,4,8]{2,1,0:T(4,128)(2,1)} reshape(bf16[4,2,28672]{2,1,0:T(2,128)(2,1)S(1)} %all-to-all-done.2) | data formatting | bytes 917504
  87.7 8.7 %copy.78 = bf16[8,4,4,1792]{3,0,2,1:T(8,128)(2,1)S(1)} copy(bf16[8,4,4,1792]{0,2,3,1:T(4,128)(2,1)} %bitcast.86) | data formatting | bytes 917504 | tf_op jit(solution)/shard_map/all_to_all | solution.py:50
  97.2 5.1 %all-to-all-start.3 = ((bf16[8,16,1792]{2,1,0:T(8,128)(2,1)}), bf16[8,16,1792]{2,1,0:T(8,128)(2,1)S(1)}, u32[]{:S(2)}, u32[]{:S(2)}) async-start(bf16[8,16,1792]{2,1,0:T(8,128)(2,1)} %copy.79), calls=%async_computation.3 | async-start | bytes 917504 | tf_op jit(solution)/shard_map/all_to_all | solution.py:49
  102.3 2.8 %fusion.32 = bf16[128,1024]{1,0:T(8,128)(2,1)S(1)} fusion(bf16[128,1792]{1,0:T(8,128)(2,1)S(1)} %bitcast.87, bf16[1,1792,1024]{2,1,0:T(8,128)(2,1)} %param.11), kind=kOutput, calls=%fused_computation.31 | convolution fusion | flops 469893120 | bytes 4390912 | tf_op jit(solution)/shard_map/dot_general | solution.py:67
  106.1 10.1 %all-to-all-done.3 = bf16[8,16,1792]{2,1,0:T(8,128)(2,1)S(1)} async-done(((bf16[8,16,1792]{2,1,0:T(8,128)(2,1)}), bf16[8,16,1792]{2,1,0:T(8,128)(2,1)S(1)}, u32[]{:S(2)}, u32[]{:S(2)}) %all-to-all-start.3) | async-done | bytes 458784 | tf_op jit(solution)/shard_map/all_to_all | solution.py:49
  116.2 2.7 %fusion.35 = bf16[128,1024]{1,0:T(8,128)(2,1)S(1)} fusion(bf16[128,1792]{1,0:T(8,128)(2,1)S(1)} %bitcast.91, bf16[1,1792,1024]{2,1,0:T(8,128)(2,1)} %param.12), kind=kOutput, calls=%fused_computation.32 | convolution fusion | flops 469893120 | bytes 4390912 | tf_op jit(solution)/shard_map/dot_general | solution.py:68
  119.9 25.7 %reduce-scatter.2.cloned.1.call-done = bf16[32,3072]{1,0:T(8,128)(2,1)} async-done(((bf16[128,3072]{1,0:T(8,128)(2,1)}), bf16[32,3072]{1,0:T(8,128)(2,1)}) %reduce-scatter.2.cloned.1.call-update) | async-done | bytes 196624 | tf_op jit(solution)/shard_map/reduce_scatter | solution.py:63
  146.6 9.1 %all_gather.10 = bf16[128,1024]{1,0:T(8,128)(2,1)S(1)} all-gather(bf16[32,1024]{1,0:T(8,128)(2,1)S(1)} %get-tuple-element.5), channel_id=1, replica_groups=mesh['dp'=4,'expert'=8] {'dp'}, dimensions={0}, use_global_device_ids=true | all-gather | bytes 327680 | tf_op jit(solution)/shard_map/all_gather | solution.py:88
  155.7 8.4 %all_gather.9 = bf16[128,1024]{1,0:T(8,128)(2,1)S(1)} all-gather(bf16[32,1024]{1,0:T(8,128)(2,1)S(1)} %get-tuple-element.6), channel_id=1, replica_groups=mesh['dp'=4,'expert'=8] {'dp'}, dimensions={0}, use_global_device_ids=true | all-gather | bytes 327680 | tf_op jit(solution)/shard_map/all_gather | solution.py:87
  164.1 9.0 %all_gather.11 = bf16[128,1024]{1,0:T(8,128)(2,1)S(1)} all-gather(bf16[32,1024]{1,0:T(8,128)(2,1)S(1)} %get-tuple-element.7), channel_id=1, replica_groups=mesh['dp'=4,'expert'=8] {'dp'}, dimensions={0}, use_global_device_ids=true | all-gather | bytes 327680 | tf_op jit(solution)/shard_map/all_gather | solution.py:89
  173.2 3.4 %fusion.21 = bf16[128,1792]{1,0:T(8,128)(2,1)S(1)} fusion(bf16[128,1024]{1,0:T(8,128)(2,1)S(1)} %all_gather.9, bf16[1,1792,1024]{2,1,0:T(8,128)(2,1)} %param.12), kind=kOutput, calls=%fused_computation.26 | convolution fusion | flops 469991424 | bytes 4390912 | tf_op jit(solution)/shard_map/dot_general | solution.py:10
  177.4 3.5 %all-to-all-start.4 = ((bf16[8,16,1792]{2,0,1:T(8,128)(2,1)}), bf16[8,16,1792]{2,0,1:T(8,128)(2,1)S(1)}, u32[]{:S(2)}, u32[]{:S(2)}) async-start(bf16[8,16,1792]{2,0,1:T(8,128)(2,1)} %copy.80), calls=%async_computation.5 | async-start | bytes 917504 | tf_op jit(solution)/shard_map/all_to_all | solution.py:105
  180.9 3.5 %fusion.7 = f32[128,1792]{1,0:T(8,128)S(1)} fusion(bf16[128,1024]{1,0:T(8,128)(2,1)S(1)} %all_gather.11, bf16[1,1792,1024]{2,1,0:T(8,128)(2,1)} %param.11), kind=kOutput, calls=%fused_computation.14 | convolution fusion | flops 469762048 | bytes 4849664 | tf_op jit(solution)/shard_map/dot_general | solution.py:10
  187.4 3.5 %all-to-all-start.6 = ((bf16[8,16,1792]{2,0,1:T(8,128)(2,1)}), bf16[8,16,1792]{2,0,1:T(8,128)(2,1)S(1)}, u32[]{:S(2)}, u32[]{:S(2)}) async-start(bf16[8,16,1792]{2,0,1:T(8,128)(2,1)} %copy.84), calls=%async_computation.7 | async-start | bytes 917504 | tf_op jit(solution)/shard_map/all_to_all | solution.py:112
  192.2 4.9 %all-to-all-done.6 = bf16[8,16,1792]{2,0,1:T(8,128)(2,1)S(1)} async-done(((bf16[8,16,1792]{2,0,1:T(8,128)(2,1)}), bf16[8,16,1792]{2,0,1:T(8,128)(2,1)S(1)}, u32[]{:S(2)}, u32[]{:S(2)}) %all-to-all-start.6) | async-done | bytes 458784 | tf_op jit(solution)/shard_map/all_to_all | solution.py:112
  197.1 4.6 %all-to-all-start.5 = ((bf16[8,4,7168]{2,1,0:T(4,128)(2,1)}), bf16[8,4,7168]{2,1,0:T(4,128)(2,1)S(1)}, u32[]{:S(2)}, u32[]{:S(2)}) async-start(bf16[8,4,7168]{2,1,0:T(4,128)(2,1)} %reshape.50), calls=%async_computation.6 | async-start | bytes 917504 | tf_op jit(solution)/shard_map/all_to_all | solution.py:104
  203.0 12.6 %all-to-all-done.5 = bf16[8,4,7168]{2,1,0:T(4,128)(2,1)S(1)} async-done(((bf16[8,4,7168]{2,1,0:T(4,128)(2,1)}), bf16[8,4,7168]{2,1,0:T(4,128)(2,1)S(1)}, u32[]{:S(2)}, u32[]{:S(2)}) %all-to-all-start.5) | async-done | bytes 458784 | tf_op jit(solution)/shard_map/all_to_all | solution.py:104
  215.7 4.1 %all-to-all-start.7 = ((bf16[8,4,7168]{2,1,0:T(4,128)(2,1)}), bf16[8,4,7168]{2,1,0:T(4,128)(2,1)}, u32[]{:S(2)}, u32[]{:S(2)}) async-start(bf16[8,4,7168]{2,1,0:T(4,128)(2,1)} %all_to_all.82), calls=%async_computation.8 | async-start | bytes 917504 | tf_op jit(solution)/shard_map/all_to_all | solution.py:111
  219.8 3.0 %fusion.17 = bf16[1,1792,1024]{2,1,0:T(8,128)(2,1)} fusion(bf16[128,1792]{1,0:T(8,128)(2,1)S(1)} %bitcast.92, bf16[128,1024]{1,0:T(8,128)(2,1)S(1)} %all_gather.9), kind=kOutput, calls=%fused_computation.24 | convolution fusion | flops 471597056 | bytes 4390912 | tf_op jit(solution)/shard_map/dot_general | solution.py:16
  222.8 3.0 %fusion.15 = bf16[1,1792,1024]{2,1,0:T(8,128)(2,1)} fusion(bf16[128,1792]{1,0:T(8,128)(2,1)S(1)} %bitcast.89, bf16[128,1024]{1,0:T(8,128)(2,1)S(1)} %all_gather.10), kind=kOutput, calls=%fused_computation.22 | convolution fusion | flops 471597056 | bytes 4390912 | tf_op jit(solution)/shard_map/dot_general | solution.py:16
  225.7 3.0 %fusion.16 = bf16[1,1792,1024]{2,1,0:T(8,128)(2,1)} fusion(bf16[128,1792]{1,0:T(8,128)(2,1)S(1)} %bitcast.90, bf16[128,1024]{1,0:T(8,128)(2,1)S(1)} %all_gather.11), kind=kOutput, calls=%fused_computation.23 | convolution fusion | flops 471597056 | bytes 4390912 | tf_op jit(solution)/shard_map/dot_general | solution.py:16
  228.7 2.9 %fusion = bf16[128,7168]{1,0:T(8,128)(2,1)} fusion(bf16[8,4,7168]{2,1,0:T(4,128)(2,1)S(1)} %all-to-all-done.5, f32[8,4]{0,1:T(4,128)S(1)} %select_reduce_fusion.1, s32[128,8]{0,1:T(8,128)S(1)} %copy.71, pred[128,8]{0,1:T(8,128)(4,1)S(1)} %copy.70), kind=kOutput, calls=%fused_computation.2 | convolution fusion | flops 353705984 | bytes 2299008 | tf_op jit(solution)/shard_map/tjc,jcd->td/dot_general | solution.py:122
  233.7 2.9 %fusion.1 = bf16[128,7168]{1,0:T(8,128)(2,1)} fusion(bf16[8,4,7168]{2,1,0:T(4,128)(2,1)} %all-to-all-done.7, s32[128,8]{0,1:T(8,128)S(1)} %copy.71, pred[128,8]{0,1:T(8,128)(4,1)S(1)} %copy.70), kind=kOutput, calls=%fused_computation.3 | convolution fusion | flops 59645952 | bytes 2298880 | tf_op jit(solution)/shard_map/tjc,jcd->td/dot_general | solution.py:125
  (45 shorter events, 15.5 us)
Async XLA Ops:
  7.2 1.5 copy-start
  16.3 15.4 %copy-start.5 = (s32[128,8]{0,1:T(8,128)S(1)}, s32[128,8]{0,1:T(8,128)}, u32[]{:S(2)}) copy-start(s32[128,8]{0,1:T(8,128)} %param.8) | copy-start | bytes 12292
  16.3 15.4 %copy-start.6 = (f32[128,8]{0,1:T(8,128)S(1)}, f32[128,8]{0,1:T(8,128)}, u32[]{:S(2)}) copy-start(f32[128,8]{0,1:T(8,128)} %param.9) | copy-start | bytes 12292
  16.3 15.5 %copy-start.4 = (bf16[128,7168]{1,0:T(8,128)(2,1)S(1)}, bf16[128,7168]{1,0:T(8,128)(2,1)}, u32[]{:S(2)}) copy-start(bf16[128,7168]{1,0:T(8,128)(2,1)} %param.13) | copy-start | bytes 5505028
  26.5 23.0 %all-to-all-start = ((bf16[4,2,28672]{2,1,0:T(2,128)(2,1)}), bf16[4,2,28672]{2,1,0:T(2,128)(2,1)S(1)}, u32[]{:S(2)}, u32[]{:S(2)}) async-start(bf16[4,2,28672]{2,1,0:T(2,128)(2,1)} %reshape.53), calls=%async_computation | async-start | bytes 917504 | tf_op jit(solution)/shard_map/all_to_all | solution.py:43
  49.5 23.5 %all-to-all-start.2 = ((bf16[4,2,28672]{2,1,0:T(2,128)(2,1)}), bf16[4,2,28672]{2,1,0:T(2,128)(2,1)S(1)}, u32[]{:S(2)}, u32[]{:S(2)}) async-start(bf16[4,2,28672]{2,1,0:T(2,128)(2,1)} %reshape.51), calls=%async_computation.2 | async-start | bytes 917504 | tf_op jit(solution)/shard_map/all_to_all | solution.py:50
  73.0 24.2 %all-to-all-start.1 = ((bf16[8,16,1792]{2,1,0:T(8,128)(2,1)}), bf16[8,16,1792]{2,1,0:T(8,128)(2,1)S(1)}, u32[]{:S(2)}, u32[]{:S(2)}) async-start(bf16[8,16,1792]{2,1,0:T(8,128)(2,1)} %copy.75), calls=%async_computation.1 | async-start | bytes 917504 | tf_op jit(solution)/shard_map/all_to_all | solution.py:42
  97.2 19.0 %all-to-all-start.3 = ((bf16[8,16,1792]{2,1,0:T(8,128)(2,1)}), bf16[8,16,1792]{2,1,0:T(8,128)(2,1)S(1)}, u32[]{:S(2)}, u32[]{:S(2)}) async-start(bf16[8,16,1792]{2,1,0:T(8,128)(2,1)} %copy.79), calls=%async_computation.3 | async-start | bytes 917504 | tf_op jit(solution)/shard_map/all_to_all | solution.py:49
  102.3 43.3 %reduce-scatter.2.cloned.1.call-start = ((), (), s32[]{:S(2)}) async-start(), calls=%async_computation.9 | async-start | bytes 983040 | tf_op jit(solution)/shard_map/reduce_scatter | solution.py:63
  102.3 3.1 %copy-start.2 = (bf16[1,1792,1024]{2,1,0:T(8,128)(2,1)S(1)}, bf16[1,1792,1024]{2,1,0:T(8,128)(2,1)}, u32[]{:S(2)}) copy-start(bf16[1,1792,1024]{2,1,0:T(8,128)(2,1)} %param.10) | copy-start | bytes 11010052
  177.4 9.9 %all-to-all-start.4 = ((bf16[8,16,1792]{2,0,1:T(8,128)(2,1)}), bf16[8,16,1792]{2,0,1:T(8,128)(2,1)S(1)}, u32[]{:S(2)}, u32[]{:S(2)}) async-start(bf16[8,16,1792]{2,0,1:T(8,128)(2,1)} %copy.80), calls=%async_computation.5 | async-start | bytes 917504 | tf_op jit(solution)/shard_map/all_to_all | solution.py:105
  180.9 3.5 %copy-start.3 = (bf16[1,1792,1024]{2,1,0:T(8,128)(2,1)S(1)}, bf16[1,1792,1024]{2,1,0:T(8,128)(2,1)}, u32[]{:S(2)}) copy-start(bf16[1,1792,1024]{2,1,0:T(8,128)(2,1)} %param.10) | copy-start | bytes 11010052
  187.4 9.8 %all-to-all-start.6 = ((bf16[8,16,1792]{2,0,1:T(8,128)(2,1)}), bf16[8,16,1792]{2,0,1:T(8,128)(2,1)S(1)}, u32[]{:S(2)}, u32[]{:S(2)}) async-start(bf16[8,16,1792]{2,0,1:T(8,128)(2,1)} %copy.84), calls=%async_computation.7 | async-start | bytes 917504 | tf_op jit(solution)/shard_map/all_to_all | solution.py:112
  197.1 18.5 %all-to-all-start.5 = ((bf16[8,4,7168]{2,1,0:T(4,128)(2,1)}), bf16[8,4,7168]{2,1,0:T(4,128)(2,1)S(1)}, u32[]{:S(2)}, u32[]{:S(2)}) async-start(bf16[8,4,7168]{2,1,0:T(4,128)(2,1)} %reshape.50), calls=%async_computation.6 | async-start | bytes 917504 | tf_op jit(solution)/shard_map/all_to_all | solution.py:104
  215.7 18.1 %all-to-all-start.7 = ((bf16[8,4,7168]{2,1,0:T(4,128)(2,1)}), bf16[8,4,7168]{2,1,0:T(4,128)(2,1)}, u32[]{:S(2)}, u32[]{:S(2)}) async-start(bf16[8,4,7168]{2,1,0:T(4,128)(2,1)} %all_to_all.82), calls=%async_computation.8 | async-start | bytes 917504 | tf_op jit(solution)/shard_map/all_to_all | solution.py:111
  222.8 13.9 %copy-start.1 = (bf16[128,7168]{1,0:T(8,128)(2,1)S(1)}, bf16[128,7168]{1,0:T(8,128)(2,1)}, u32[]{:S(2)}) copy-start(bf16[128,7168]{1,0:T(8,128)(2,1)} %param.7) | copy-start | bytes 5505028
Sparse Core Ops, SparseCore 0:
  120.0 25.5 reduce-scatter.1
where the time goes:
time: 245 us; the launch traced here: 243 us
  local copies, waits for them, and re-layouts  78.5 us (32%)
  waiting for transfers between devices  56.1 us (23%)
  starting transfers between devices  35.1 us (14%)
  matrix products  29.9 us (12%)
  blocking collectives  26.5 us (11%)
  between operations  14.2 us (6%)
  other arithmetic  3.11 us (1%)
    unnamed x18, local copies, waits for them, and re-layouts  40.4 us
    reduce_scatter x1, waiting for transfers between devices, body(): lax.psum_scatter(jnp.concatenate([jnp.dot(row_block, gate_mat, preferred_...  25.7 us
    all_to_all x1, waiting for transfers between devices, body(): lax.all_to_all(lax.all_to_all(out_rows.reshape(layout), 'dp', split_axis=...  12.6 us
    all_to_all x1, waiting for transfers between devices, body(): lax.all_to_all(lax.all_to_all(send_grads, 'dp', split_axis=2, concat_axis...  10.1 us
    all_to_all x2, local copies, waits for them, and re-layouts, body(): lax.all_to_all(send_rows, 'dp', split_axis=2, concat_axis=1, tiled=True)  9.54 us
    all_to_all x2, local copies, waits for them, and re-layouts, body(): lax.all_to_all(send_grads, 'dp', split_axis=2, concat_axis=1, tiled=True)  9.54 us
    all_gather x1, blocking collectives, body(): gate_part = lax.all_gather(gate_grad, 'dp', axis=0, tiled=True)  9.05 us
    all_gather x1, blocking collectives, body(): up_part = lax.all_gather(up_grad, 'dp', axis=0, tiled=True)  9.04 us
  transfers between devices with their start and end apart: 9, of which 6 were waited for; matrix products, arithmetic and copies ran while one was open for 33% of the time, Pallas kernels for 0%

commit v1 on v0

--- a/solution.py
+++ b/solution.py
@@ -4,6 +4,28 @@
 from jax.sharding import PartitionSpec as P
 
 CAP = 4
+
+
+def time_side_here(here_x, across, array_dim, out_dim):
+    known = lax.axis_size(across)
+    local_out = lax.axis_index(across)
+    everything, next_value = (known, local_out)
+    d_next = here_x.shape[array_dim] // everything
+    later = list(here_x.shape)
+    later[array_dim] = d_next
+    g_now = later[out_dim]
+    later[out_dim] = g_now * everything
+    built = jnp.zeros(later, here_x.dtype)
+    for src_i in [*range(everything)]:
+        x_now = lax.dynamic_slice_in_dim(
+            here_x, (next_value ^ src_i) * d_next, d_next, axis=array_dim
+        )
+        if src_i:
+            x_now = lax.ppermute(x_now, across, [(rr, rr ^ src_i) for rr in range(everything)])
+        built = lax.dynamic_update_slice_in_dim(
+            built, x_now, (next_value ^ src_i) * g_now, axis=out_dim
+        )
+    return built
 
 
 def contract_last(left, right):
@@ -47,7 +69,7 @@
             tiled=True,
         ),
         lax.all_to_all(
-            lax.all_to_all(send_grads, "dp", split_axis=2, concat_axis=1, tiled=True),
+            time_side_here(send_grads, "dp", 2, 1),
             "expert",
             split_axis=0,
             concat_axis=0,

time: 245 us -> 219 us (0.89)
  local copies, waits for them, and re-layouts: 78.5 us -> 50.8 us
  waiting for transfers between devices: 56.1 us -> 52.4 us
    unnamed x18 -> x8, local copies, waits for them, and re-layouts: 40.4 us -> 20.2 us
    all_to_all x1, waiting for transfers between devices: 0.01 us -> 11.2 us  [body(): lax.all_to_all(lax.all_to_all(send_rows, 'dp', split_axis=2, concat_axis=...]
    all_to_all x1, waiting for transfers between devices: 12.6 us -> 2.06 us  [body(): lax.all_to_all(lax.all_to_all(out_rows.reshape(layout), 'dp', split_axis=...]
    all_to_all x2 -> x1, waiting for transfers between devices: 10.1 us -> 0.01 us  [body(): lax.all_to_all(time_side_here(send_grads, 'dp', 2, 1), 'expert', split_ax...]
    all_to_all x2 -> x0, local copies, waits for them, and re-layouts: 9.54 us -> none  [body(): lax.all_to_all(send_grads, 'dp', split_axis=2, concat_axis=1, tiled=True)]
    all_to_all x1, waiting for transfers between devices: 2.05 us -> 9.93 us  [body(): lax.all_to_all(lax.all_to_all(input_rows.reshape(layout), 'dp', split_axi...]
    convert_element_type x1 -> x0, local copies, waits for them, and re-layouts: 7.2 us -> none  [body(): send_grads = (slot_gate[:, :, None] * picked).astype(jnp.bfloat16)]
    all_to_all x1, waiting for transfers between devices: 4.93 us -> 0.01 us  [body(): lax.all_to_all(input_rows.reshape(layout), 'dp', split_axis=1, concat_axi...]
  transfers between devices with their start and end apart: 9 -> 11, of which waited for: 6 -> 6; matrix products, arithmetic and copies ran while one was open for 33% -> 31% of each run, Pallas kernels for 0% -> 0%
where the time goes in v1:
time: 219 us; the launch traced here: 218 us
  waiting for transfers between devices  52.4 us (24%)
  local copies, waits for them, and re-layouts  50.8 us (23%)
  starting transfers between devices  35.9 us (16%)
  matrix products  32.3 us (15%)
  blocking collectives  27.6 us (13%)
  between operations  14.2 us (6%)
  other arithmetic  4.6 us (2%)
    reduce_scatter x1, waiting for transfers between devices, body(): lax.psum_scatter(jnp.concatenate([jnp.dot(row_block, gate_mat, preferred_...  24.3 us
    unnamed x8, local copies, waits for them, and re-layouts  20.2 us
    all_to_all x1, waiting for transfers between devices, body(): lax.all_to_all(lax.all_to_all(send_rows, 'dp', split_axis=2, concat_axis=...  11.2 us
    all_gather x1, blocking collectives, body(): hidden_part = lax.all_gather(hidden, 'dp', axis=0, tiled=True)  10.7 us
    all_to_all x1, waiting for transfers between devices, body(): lax.all_to_all(lax.all_to_all(input_rows.reshape(layout), 'dp', split_axi...  9.93 us
    all_to_all x2, local copies, waits for them, and re-layouts, body(): lax.all_to_all(send_rows, 'dp', split_axis=2, concat_axis=1, tiled=True)  9.54 us
    all_gather x1, blocking collectives, body(): up_part = lax.all_gather(up_grad, 'dp', axis=0, tiled=True)  9.06 us
    dot_general x3, matrix products, contract_first(): lax.dot_general(left, right, (((0,), (0,)), ((), ())), preferred_element_...  8.94 us
  transfers between devices with their start and end apart: 11, of which 6 were waited for; matrix products, arithmetic and copies ran while one was open for 31% of the time, Pallas kernels for 0%

profile of v1, /device:TPU:0, one launch (start us, length us, event | category | flops | bytes accessed | tf_op | source)
XLA Modules:
  0.0 217.8 jit_solution(6660374598911541907)
XLA Ops:
  9.8 3.0 %collective-permute-start = (bf16[8,4,1792]{2,0,1:T(8,128)(2,1)S(1)}, bf16[8,4,1792]{2,0,1:T(8,128)(2,1)S(1)}, u32[]{:S(2)}, u32[]{:S(2)}) collective-permute-start(bf16[8,4,1792]{2,0,1:T(8,128)(2,1)S(1)} %get-tuple-element.7), channel_id=1, source_target_pairs={{0,8},{8,0},{16,24},{24,16},{1,9},{9,1},{17,25},{25,17},{2,10},{10... | collective-permute-start | bytes 344072 | tf_op jit(solution)/shard_map/ppermute | solution.py:24
  16.2 7.2 %copy.79 = bf16[8,4,7168]{0,1,2:T(4,128)(2,1)} copy(bf16[8,4,7168]{2,0,1:T(8,128)(2,1)S(1)} %convolution_convert_fusion) | data formatting | bytes 917504 | tf_op jit(solution)/shard_map/convert_element_type | solution.py:60
  23.4 10.1 %reshape.51 = bf16[4,2,28672]{2,1,0:T(2,128)(2,1)} reshape(bf16[7168,4,8]{2,1,0:T(4,128)(2,1)} %bitcast.76) | data formatting | bytes 917504
  33.5 4.2 %all-to-all-start = ((bf16[4,2,28672]{2,1,0:T(2,128)(2,1)}), bf16[4,2,28672]{2,1,0:T(2,128)(2,1)S(1)}, u32[]{:S(2)}, u32[]{:S(2)}) async-start(bf16[4,2,28672]{2,1,0:T(2,128)(2,1)} %reshape.51), calls=%async_computation | async-start | bytes 917504 | tf_op jit(solution)/shard_map/all_to_all | solution.py:65
  41.2 2.9 %all-to-all-done = bf16[4,2,28672]{2,1,0:T(2,128)(2,1)S(1)} async-done(((bf16[4,2,28672]{2,1,0:T(2,128)(2,1)}), bf16[4,2,28672]{2,1,0:T(2,128)(2,1)S(1)}, u32[]{:S(2)}, u32[]{:S(2)}) %all-to-all-start) | async-done | bytes 458784 | tf_op jit(solution)/shard_map/all_to_all | solution.py:65
  44.1 4.9 %all-to-all-start.2 = ((bf16[8,16,1792]{2,1,0:T(8,128)(2,1)}), bf16[8,16,1792]{2,1,0:T(8,128)(2,1)S(1)}, u32[]{:S(2)}, u32[]{:S(2)}) async-start(bf16[8,16,1792]{2,1,0:T(8,128)(2,1)} %copy_dynamic-update-slice_fusion), calls=%async_computation.2 | async-start | bytes 917504 | tf_op jit(solution)/shard_map/all_to_all | solution.py:71
  49.0 9.8 %reshape.52 = bf16[7168,4,8]{2,1,0:T(4,128)(2,1)} reshape(bf16[4,2,28672]{2,1,0:T(2,128)(2,1)S(1)} %all-to-all-done) | data formatting | bytes 917504
  58.8 8.7 %copy.81 = bf16[8,4,4,1792]{3,0,2,1:T(8,128)(2,1)S(1)} copy(bf16[8,4,4,1792]{0,2,3,1:T(4,128)(2,1)} %bitcast.77) | data formatting | bytes 917504 | tf_op jit(solution)/shard_map/all_to_all | solution.py:65
  68.4 5.1 %all-to-all-start.1 = ((bf16[8,16,1792]{2,1,0:T(8,128)(2,1)}), bf16[8,16,1792]{2,1,0:T(8,128)(2,1)S(1)}, u32[]{:S(2)}, u32[]{:S(2)}) async-start(bf16[8,16,1792]{2,1,0:T(8,128)(2,1)} %copy.82), calls=%async_computation.1 | async-start | bytes 917504 | tf_op jit(solution)/shard_map/all_to_all | solution.py:64
  73.5 2.7 %fusion.35 = bf16[128,1024]{1,0:T(8,128)(2,1)S(1)} fusion(bf16[128,1792]{1,0:T(8,128)(2,1)S(1)} %bitcast.82, bf16[1,1792,1024]{2,1,0:T(8,128)(2,1)} %param.12), kind=kOutput, calls=%fused_computation.32 | convolution fusion | flops 469893120 | bytes 4390912 | tf_op jit(solution)/shard_map/dot_general | solution.py:90
  76.2 11.2 %all-to-all-done.1 = bf16[8,16,1792]{2,1,0:T(8,128)(2,1)S(1)} async-done(((bf16[8,16,1792]{2,1,0:T(8,128)(2,1)}), bf16[8,16,1792]{2,1,0:T(8,128)(2,1)S(1)}, u32[]{:S(2)}, u32[]{:S(2)}) %all-to-all-start.1) | async-done | bytes 458784 | tf_op jit(solution)/shard_map/all_to_all | solution.py:64
  87.4 2.8 %fusion.29 = bf16[128,1024]{1,0:T(8,128)(2,1)S(1)} fusion(bf16[128,1792]{1,0:T(8,128)(2,1)S(1)} %bitcast.78, bf16[1,1792,1024]{2,1,0:T(8,128)(2,1)} %param.10), kind=kOutput, calls=%fused_computation.30 | convolution fusion | flops 469893120 | bytes 4390912 | tf_op jit(solution)/shard_map/dot_general | solution.py:88
  92.1 24.3 %reduce-scatter.2.cloned.1.call-done = bf16[32,3072]{1,0:T(8,128)(2,1)} async-done(((bf16[128,3072]{1,0:T(8,128)(2,1)}), bf16[32,3072]{1,0:T(8,128)(2,1)}) %reduce-scatter.2.cloned.1.call-update) | async-done | bytes 196624 | tf_op jit(solution)/shard_map/reduce_scatter | solution.py:85
  118.2 9.1 %all_gather.11 = bf16[128,1024]{1,0:T(8,128)(2,1)S(1)} all-gather(bf16[32,1024]{1,0:T(8,128)(2,1)S(1)} %get-tuple-element.11), channel_id=1, replica_groups=mesh['dp'=4,'expert'=8] {'dp'}, dimensions={0}, use_global_device_ids=true | all-gather | bytes 327680 | tf_op jit(solution)/shard_map/all_gather | solution.py:111
  127.3 7.9 %all_gather.10 = bf16[128,1024]{1,0:T(8,128)(2,1)S(1)} all-gather(bf16[32,1024]{1,0:T(8,128)(2,1)S(1)} %get-tuple-element.9), channel_id=1, replica_groups=mesh['dp'=4,'expert'=8] {'dp'}, dimensions={0}, use_global_device_ids=true | all-gather | bytes 327680 | tf_op jit(solution)/shard_map/all_gather | solution.py:110
  135.2 3.4 %fusion.7 = f32[128,1792]{1,0:T(8,128)S(1)} fusion(bf16[128,1024]{1,0:T(8,128)(2,1)S(1)} %all_gather.11, bf16[1,1792,1024]{2,1,0:T(8,128)(2,1)} %param.11), kind=kOutput, calls=%fused_computation.14 | convolution fusion | flops 469762048 | bytes 4849664 | tf_op jit(solution)/shard_map/dot_general | solution.py:32
  140.8 4.1 %all-to-all-start.5 = ((bf16[8,16,1792]{2,0,1:T(8,128)(2,1)}), bf16[8,16,1792]{2,0,1:T(8,128)(2,1)}, u32[]{:S(2)}, u32[]{:S(2)}) async-start(bf16[8,16,1792]{2,0,1:T(8,128)(2,1)} %copy.91), calls=%async_computation.6 | async-start | bytes 917504 | tf_op jit(solution)/shard_map/all_to_all | solution.py:134
  145.0 10.7 %all_gather.9 = bf16[128,1024]{1,0:T(8,128)(2,1)S(1)} all-gather(bf16[32,1024]{1,0:T(8,128)(2,1)} %get-tuple-element.10), channel_id=1, replica_groups=mesh['dp'=4,'expert'=8] {'dp'}, dimensions={0}, use_global_device_ids=true | all-gather | bytes 327680 | tf_op jit(solution)/shard_map/all_gather | solution.py:109
  155.6 3.4 %fusion.21 = bf16[128,1792]{1,0:T(8,128)(2,1)S(1)} fusion(bf16[128,1024]{1,0:T(8,128)(2,1)S(1)} %all_gather.9, bf16[1,1792,1024]{2,1,0:T(8,128)(2,1)} %param.12), kind=kOutput, calls=%fused_computation.26 | convolution fusion | flops 469991424 | bytes 4390912 | tf_op jit(solution)/shard_map/dot_general | solution.py:32
  159.9 4.3 %all-to-all-start.3 = ((bf16[8,16,1792]{2,0,1:T(8,128)(2,1)}), bf16[8,16,1792]{2,0,1:T(8,128)(2,1)}, u32[]{:S(2)}, u32[]{:S(2)}) async-start(bf16[8,16,1792]{2,0,1:T(8,128)(2,1)} %copy.87), calls=%async_computation.4 | async-start | bytes 917504 | tf_op jit(solution)/shard_map/all_to_all | solution.py:127
  164.2 2.1 copy.92
  168.3 2.0 all-to-all-done.3
  170.3 4.6 %all-to-all-start.6 = ((bf16[8,4,7168]{2,1,0:T(4,128)(2,1)}), bf16[8,4,7168]{2,1,0:T(4,128)(2,1)}, u32[]{:S(2)}, u32[]{:S(2)}) async-start(bf16[8,4,7168]{2,1,0:T(4,128)(2,1)} %all_to_all.65), calls=%async_computation.7 | async-start | bytes 917504 | tf_op jit(solution)/shard_map/all_to_all | solution.py:133
  174.9 2.1 copy.96
  179.0 9.9 %all-to-all-done.6 = bf16[8,4,7168]{2,1,0:T(4,128)(2,1)} async-done(((bf16[8,4,7168]{2,1,0:T(4,128)(2,1)}), bf16[8,4,7168]{2,1,0:T(4,128)(2,1)}, u32[]{:S(2)}, u32[]{:S(2)}) %all-to-all-start.6) | async-done | bytes 458784 | tf_op jit(solution)/shard_map/all_to_all | solution.py:133
  189.0 4.1 %all-to-all-start.4 = ((bf16[8,4,7168]{2,1,0:T(4,128)(2,1)}), bf16[8,4,7168]{2,1,0:T(4,128)(2,1)}, u32[]{:S(2)}, u32[]{:S(2)}) async-start(bf16[8,4,7168]{2,1,0:T(4,128)(2,1)} %reshape.50), calls=%async_computation.5 | async-start | bytes 917504 | tf_op jit(solution)/shard_map/all_to_all | solution.py:126
  193.1 3.0 %fusion.16 = bf16[1,1792,1024]{2,1,0:T(8,128)(2,1)} fusion(bf16[128,1792]{1,0:T(8,128)(2,1)S(1)} %bitcast.80, bf16[128,1024]{1,0:T(8,128)(2,1)S(1)} %all_gather.11), kind=kOutput, calls=%fused_computation.23 | convolution fusion | flops 471597056 | bytes 4390912 | tf_op jit(solution)/shard_map/dot_general | solution.py:38
  196.1 3.0 %fusion.15 = bf16[1,1792,1024]{2,1,0:T(8,128)(2,1)} fusion(bf16[128,1792]{1,0:T(8,128)(2,1)S(1)} %bitcast.81, bf16[128,1024]{1,0:T(8,128)(2,1)S(1)} %all_gather.10), kind=kOutput, calls=%fused_computation.22 | convolution fusion | flops 471597056 | bytes 4390912 | tf_op jit(solution)/shard_map/dot_general | solution.py:38
  199.0 3.0 %fusion.17 = bf16[1,1792,1024]{2,1,0:T(8,128)(2,1)} fusion(bf16[128,1792]{1,0:T(8,128)(2,1)S(1)} %bitcast.83, bf16[128,1024]{1,0:T(8,128)(2,1)S(1)} %all_gather.9), kind=kOutput, calls=%fused_computation.24 | convolution fusion | flops 471597056 | bytes 4390912 | tf_op jit(solution)/shard_map/dot_general | solution.py:38
  202.0 2.9 %fusion.1 = bf16[128,7168]{1,0:T(8,128)(2,1)} fusion(bf16[8,4,7168]{2,1,0:T(4,128)(2,1)} %all-to-all-done.6, s32[128,8]{0,1:T(8,128)S(1)} %copy.78, pred[128,8]{0,1:T(8,128)(4,1)S(1)} %copy.77), kind=kOutput, calls=%fused_computation.3 | convolution fusion | flops 59645952 | bytes 2298880 | tf_op jit(solution)/shard_map/tjc,jcd->td/dot_general | solution.py:147
  205.0 2.1 all-to-all-done.4
  207.0 3.9 %fusion = bf16[128,7168]{1,0:T(8,128)(2,1)} fusion(bf16[8,4,7168]{2,1,0:T(4,128)(2,1)} %all-to-all-done.4, f32[8,4]{0,1:T(4,128)S(1)} %select_reduce_fusion.1, s32[128,8]{0,1:T(8,128)S(1)} %copy.78, pred[128,8]{0,1:T(8,128)(4,1)S(1)} %copy.77), kind=kOutput, calls=%fused_computation.2 | convolution fusion | flops 353705984 | bytes 2299008 | tf_op jit(solution)/shard_map/tjc,jcd->td/dot_general | solution.py:144
  (42 shorter events, 21.2 us)
Async XLA Ops:
  7.2 2.2 copy-start
  9.8 29.4 %collective-permute-start = (bf16[8,4,1792]{2,0,1:T(8,128)(2,1)S(1)}, bf16[8,4,1792]{2,0,1:T(8,128)(2,1)S(1)}, u32[]{:S(2)}, u32[]{:S(2)}) collective-permute-start(bf16[8,4,1792]{2,0,1:T(8,128)(2,1)S(1)} %get-tuple-element.7), channel_id=1, source_target_pairs={{0,8},{8,0},{16,24},{24,16},{1,9},{9,1},{17,25},{25,17},{2,10},{10... | collective-permute-start | bytes 344072 | tf_op jit(solution)/shard_map/ppermute | solution.py:24
  12.8 27.1 %collective-permute-start.1 = (bf16[8,4,1792]{2,0,1:T(8,128)(2,1)S(1)}, bf16[8,4,1792]{2,0,1:T(8,128)(2,1)S(1)}, u32[]{:S(2)}, u32[]{:S(2)}) collective-permute-start(bf16[8,4,1792]{2,0,1:T(8,128)(2,1)S(1)} %get-tuple-element.6), channel_id=1, source_target_pairs={{0,16},{8,24},{16,0},{24,8},{1,17},{9,25},{17,1},{25,9},{2,18},{10... | collective-permute-start | bytes 344072 | tf_op jit(solution)/shard_map/ppermute | solution.py:24
  14.3 26.2 %collective-permute-start.2 = (bf16[8,4,1792]{2,0,1:T(8,128)(2,1)S(1)}, bf16[8,4,1792]{2,0,1:T(8,128)(2,1)S(1)}, u32[]{:S(2)}, u32[]{:S(2)}) collective-permute-start(bf16[8,4,1792]{2,0,1:T(8,128)(2,1)S(1)} %get-tuple-element.5), channel_id=1, source_target_pairs={{0,24},{8,16},{16,8},{24,0},{1,25},{9,17},{17,9},{25,1},{2,26},{10... | collective-permute-start | bytes 344072 | tf_op jit(solution)/shard_map/ppermute | solution.py:24
  33.5 10.6 %all-to-all-start = ((bf16[4,2,28672]{2,1,0:T(2,128)(2,1)}), bf16[4,2,28672]{2,1,0:T(2,128)(2,1)S(1)}, u32[]{:S(2)}, u32[]{:S(2)}) async-start(bf16[4,2,28672]{2,1,0:T(2,128)(2,1)} %reshape.51), calls=%async_computation | async-start | bytes 917504 | tf_op jit(solution)/shard_map/all_to_all | solution.py:65
  44.1 24.3 %all-to-all-start.2 = ((bf16[8,16,1792]{2,1,0:T(8,128)(2,1)}), bf16[8,16,1792]{2,1,0:T(8,128)(2,1)S(1)}, u32[]{:S(2)}, u32[]{:S(2)}) async-start(bf16[8,16,1792]{2,1,0:T(8,128)(2,1)} %copy_dynamic-update-slice_fusion), calls=%async_computation.2 | async-start | bytes 917504 | tf_op jit(solution)/shard_map/all_to_all | solution.py:71
  68.4 19.0 %all-to-all-start.1 = ((bf16[8,16,1792]{2,1,0:T(8,128)(2,1)}), bf16[8,16,1792]{2,1,0:T(8,128)(2,1)S(1)}, u32[]{:S(2)}, u32[]{:S(2)}) async-start(bf16[8,16,1792]{2,1,0:T(8,128)(2,1)} %copy.82), calls=%async_computation.1 | async-start | bytes 917504 | tf_op jit(solution)/shard_map/all_to_all | solution.py:64
  73.5 43.0 %reduce-scatter.2.cloned.1.call-start = ((), (), s32[]{:S(2)}) async-start(), calls=%async_computation.8 | async-start | bytes 983040 | tf_op jit(solution)/shard_map/reduce_scatter | solution.py:85
  87.4 3.1 %copy-start.1 = (bf16[1,1792,1024]{2,1,0:T(8,128)(2,1)S(1)}, bf16[1,1792,1024]{2,1,0:T(8,128)(2,1)}, u32[]{:S(2)}) copy-start(bf16[1,1792,1024]{2,1,0:T(8,128)(2,1)} %param.11) | copy-start | bytes 11010052
  116.4 22.2 %copy-start.2 = (bf16[1,1792,1024]{2,1,0:T(8,128)(2,1)S(1)}, bf16[1,1792,1024]{2,1,0:T(8,128)(2,1)}, u32[]{:S(2)}) copy-start(bf16[1,1792,1024]{2,1,0:T(8,128)(2,1)} %param.10) | copy-start | bytes 11010052
  140.8 19.1 %all-to-all-start.5 = ((bf16[8,16,1792]{2,0,1:T(8,128)(2,1)}), bf16[8,16,1792]{2,0,1:T(8,128)(2,1)}, u32[]{:S(2)}, u32[]{:S(2)}) async-start(bf16[8,16,1792]{2,0,1:T(8,128)(2,1)} %copy.91), calls=%async_computation.6 | async-start | bytes 917504 | tf_op jit(solution)/shard_map/all_to_all | solution.py:134
  159.9 10.4 %all-to-all-start.3 = ((bf16[8,16,1792]{2,0,1:T(8,128)(2,1)}), bf16[8,16,1792]{2,0,1:T(8,128)(2,1)}, u32[]{:S(2)}, u32[]{:S(2)}) async-start(bf16[8,16,1792]{2,0,1:T(8,128)(2,1)} %copy.87), calls=%async_computation.4 | async-start | bytes 917504 | tf_op jit(solution)/shard_map/all_to_all | solution.py:127
  170.3 18.6 %all-to-all-start.6 = ((bf16[8,4,7168]{2,1,0:T(4,128)(2,1)}), bf16[8,4,7168]{2,1,0:T(4,128)(2,1)}, u32[]{:S(2)}, u32[]{:S(2)}) async-start(bf16[8,4,7168]{2,1,0:T(4,128)(2,1)} %all_to_all.65), calls=%async_computation.7 | async-start | bytes 917504 | tf_op jit(solution)/shard_map/all_to_all | solution.py:133
  189.0 18.1 %all-to-all-start.4 = ((bf16[8,4,7168]{2,1,0:T(4,128)(2,1)}), bf16[8,4,7168]{2,1,0:T(4,128)(2,1)}, u32[]{:S(2)}, u32[]{:S(2)}) async-start(bf16[8,4,7168]{2,1,0:T(4,128)(2,1)} %reshape.50), calls=%async_computation.5 | async-start | bytes 917504 | tf_op jit(solution)/shard_map/all_to_all | solution.py:126
Sparse Core Ops, SparseCore 0:
  92.3 24.1 reduce-scatter.1
